TPU v7x, 128 devices: a whole 4x4x4 slice. The times are simulated.
128 devices in a mesh: mode: 8 (over x_hi, z), tile: 16 (over y, x_lo, core).
Axes of the slice: x: 4 (x_hi: 2, x_lo: 2; x = x_hi * 2 + x_lo), y: 4, z: 4, core: 2. Of those that a mesh axis runs over, the one named last changes fastest.
Arguments:
- distribution: float32 [4096, 128, 128], P('mode', 'tile'), may hold values from -6 to 6
- courant: float32 [2, 4096], P(None, 'mode'), may hold values from -0.4 to 0.4
- relax_rate: float32 [4096], P('mode'), may hold values from 0.1 to 2
- scatter_weight: float32 [4096, 4096], P('mode'), may hold values from -0.09375 to 0.09375
- cell_flags: int32 [128, 128], P('tile'), may hold values 0 or 1
Outputs:
- evolved: float32 [4096, 128, 128], P('mode', 'tile')
All inputs are finite; a program needn't handle non-finite values. No bound on the sum of `cell_flags` on one device may be relied on, other than what follows from the above.
Results may differ from a plain program's by a relative error of at most 0.0012.
Values may be sent and summed in bfloat16 or wider, within the bound.
A program may use at most 128 MiB of HBM per device.

v0:
```python
import jax
import jax.numpy as jnp
from jax import lax
from jax.sharding import PartitionSpec as P

time_step = 0.25
wall_rate = 2.0


def extended(block, sides, width):
    for axis, dim in sides:
        count = lax.axis_size(axis)
        forward = [(i, i + 1) for i in range(count - 1)]
        backward = [(target, source) for source, target in forward]
        low = lax.ppermute(
            lax.slice_in_dim(block, block.shape[dim] - width, None, axis=dim), axis, forward
        )
        high = lax.ppermute(lax.slice_in_dim(block, 0, width, axis=dim), axis, backward)
        block = jnp.concatenate([low, block, high], axis=dim)
    return block


def transport_rows(padded, cx, cy):
    full = jnp.pad(padded, ((0, 0), (0, 0), (2, 2)))
    centre = full[:, 2:-2, 2:-2]
    back_x = 1.5 * centre - 2.0 * full[:, 1:-3, 2:-2] + 0.5 * full[:, :-4, 2:-2]
    fwd_x = -1.5 * centre + 2.0 * full[:, 3:-1, 2:-2] - 0.5 * full[:, 4:, 2:-2]
    back_y = 1.5 * centre - 2.0 * full[:, 2:-2, 1:-3] + 0.5 * full[:, 2:-2, :-4]
    fwd_y = -1.5 * centre + 2.0 * full[:, 2:-2, 3:-1] - 0.5 * full[:, 2:-2, 4:]
    return (
        jnp.maximum(cx, 0.0) * back_x
        + jnp.minimum(cx, 0.0) * fwd_x
        + jnp.maximum(cy, 0.0) * back_y
        + jnp.minimum(cy, 0.0) * fwd_y
    )


def collide(field, scatter_weight):
    rounded = field.astype(jnp.bfloat16)
    count = rounded.shape[1] * rounded.shape[2]
    flat = rounded.reshape(rounded.shape[0], count)
    gain = jnp.dot(
        scatter_weight,
        lax.all_gather(flat, "mode", axis=0, tiled=True).astype(jnp.float32),
        precision=lax.Precision.HIGHEST,
        preferred_element_type=jnp.float32,
    )
    return gain.reshape(field.shape)


def update(centre, moved, gain, rate, flags):
    return centre - moved + time_step * (gain - rate * centre - wall_rate * flags * centre)


def body(distribution, courant, relax_rate, scatter_weight, cell_flags):
    cx = courant[0][:, None, None]
    cy = courant[1][:, None, None]
    rate = relax_rate[:, None, None]
    flags = cell_flags.astype(jnp.float32)[None]
    field = distribution
    for step in range(2):
        padded = extended(field, (("tile", 1),), 2)
        moved = transport_rows(padded, cx, cy)
        gain = collide(field, scatter_weight)
        field = update(field, moved, gain, rate, flags)
    return field


def solution(mesh):
    in_specs = (
        P("mode", "tile", None),
        P(None, "mode"),
        P("mode"),
        P("mode", None),
        P("tile", None),
    )
    out_specs = P("mode", "tile", None)
    return jax.shard_map(body, mesh=mesh, in_specs=in_specs, out_specs=out_specs, check_vma=False)
```

profile of v0, /device:TPU:0, one launch (start us, length us, event | category | flops | bytes accessed | tf_op | source)
XLA Modules:
  0.0 288.8 jit_solution(3713576620583982703)
XLA Ops:
  6.5 1.7 convert_element_type.14
  8.2 1.3 copy.47
  9.6 0.6 copy-done.2
  10.2 0.3 fusion.50
  10.6 1.3 collective-permute-start.1
  11.9 0.9 copy.43
  12.7 4.0 %collective-permute-start = (f32[512,2,128]{2,0,1:T(8,128)}, f32[512,2,128]{2,0,1:T(8,128)}, u32[]{:S(2)}, u32[]{:S(2)}) collective-permute-start(f32[512,2,128]{2,0,1:T(8,128)} %copy.43), channel_id=1, source_target_pairs={{0,1},{1,2},{2,3},{3,4},{4,5},{5,6},{6,7},{7,8},{8,9},{9,10},{10,1... | collective-permute-start | bytes 1572872 | tf_op jit(solution)/shard_map/ppermute | solution.py:15
  16.7 1.8 copy.31
  18.5 1.0 copy.27
  19.6 2.1 copy.22
  21.6 2.7 select_maximum_fusion.2
  24.4 98.0 %all-gather.3.cloned.1.call-done = bf16[4096,1024]{1,0:T(8,128)(2,1)} async-done(((bf16[512,1024]{1,0:T(8,128)(2,1)}), bf16[4096,1024]{1,0:T(8,128)(2,1)}) %all-gather.3.cloned.1.call-update) | async-done | bytes 8388624 | tf_op jit(solution)/shard_map/all_gather | solution.py:44
  122.4 16.5 %fusion.51 = f32[512,1024]{0,1:T(8,128)S(1)} fusion(f32[512,4096]{1,0:T(8,128)} %param.8, bf16[4096,1024]{1,0:T(8,128)(2,1)} %all-gather.3.cloned.1.call-done), kind=kOutput, calls=%fused_computation.82 | convolution fusion | flops 25769803776 | bytes 18874368 | tf_op jit(solution)/shard_map/reshape | solution.py:48
  139.0 3.9 %fusion.47 = (bf16[512,8,128]{0,2,1:T(8,128)(2,1)}, f32[512,8,128]{0,2,1:T(8,128)}) fusion(f32[512,8,128]{0,2,1:T(8,128)S(1)} %copy-done.1, f32[8,128]{1,0:T(8,128)S(1)} %convert_multiply_fusion, f32[512,8,128]{0,2,1:T(8,128)S(1)} %bitcast.21, f32[512]{0:T(512)S(1)} %copy-done.7, f32[512,12,132]{0,2,1:T(8,128)S(1)} %select_maximum_fusion.2, ...), kind=kLoop, calls=%fused_computation.79 | loop fusion | flops 19398656 | bytes 16791552 | tf_op jit(solution)/shard_map/convert_element_type | solution.py:39
  142.9 1.3 fusion.49
  144.4 1.3 collective-permute-start.3
  145.9 3.2 %collective-permute-start.2 = (f32[512,2,128]{2,0,1:T(8,128)S(1)}, f32[512,2,128]{2,0,1:T(8,128)S(1)}, u32[]{:S(2)}, u32[]{:S(2)}) collective-permute-start(f32[512,2,128]{2,0,1:T(8,128)S(1)} %copy.35), channel_id=1, source_target_pairs={{0,1},{1,2},{2,3},{3,4},{4,5},{5,6},{6,7},{7,8},{8,9},{9,10},{10,1... | collective-permute-start | bytes 1572872 | tf_op jit(solution)/shard_map/ppermute | solution.py:15
  149.2 1.0 copy.38
  150.5 1.0 copy.36
  151.5 2.5 select_maximum_fusion
  154.0 104.8 %all-gather.5.cloned.1.call-done = bf16[4096,1024]{0,1:T(8,128)(2,1)} async-done(((bf16[512,1024]{0,1:T(8,128)(2,1)}), bf16[4096,1024]{0,1:T(8,128)(2,1)}) %all-gather.5.cloned.1.call-update) | async-done | bytes 8388624 | tf_op jit(solution)/shard_map/all_gather | solution.py:44
  258.8 16.6 %fusion.52 = f32[1024,512]{1,0:T(8,128)S(1)} fusion(bf16[4096,1024]{0,1:T(8,128)(2,1)} %all-gather.5.cloned.1.call-done, f32[512,4096]{1,0:T(8,128)} %param.8), kind=kOutput, calls=%fused_computation.83 | convolution fusion | flops 25769803776 | bytes 18874368 | tf_op jit(solution)/shard_map/dot_general | solution.py:42
  275.4 3.7 %fusion.10 = f32[512,8,128]{0,2,1:T(8,128)} fusion(f32[512,8,128]{0,2,1:T(8,128)S(1)} %copy-done, f32[512,2,128]{0,2,1:T(8,128)S(1)} %copy-done.3, f32[512,2,128]{0,2,1:T(8,128)S(1)} %copy-done.5, f32[512,12,132]{0,2,1:T(8,128)S(1)} %select_maximum_fusion, f32[512,8,128]{0,2,1:T(8,128)S(1)} %bitcast.20, f32[8,128]{1,0:T(8,128)S(1)} %convert_multiply_fusion, ...), kind=kLoop, calls=%fused_computation.24 | loop fusion | flops 18874368 | bytes 15742976 | tf_op jit(solution)/shard_map/add | solution.py:52
  279.1 2.9 %copy.41 = f32[512,8,128]{2,1,0:T(8,128)} copy(f32[512,8,128]{0,2,1:T(8,128)} %fusion.10) | data formatting | bytes 4194304 | tf_op jit(solution)/shard_map/add | solution.py:52
  (32 shorter events, 0.9 us)
Async XLA Ops:
  6.5 115.9 %all-gather.3.cloned.1.call-start = ((), (), s32[]{:S(2)}) async-start(), calls=%async_computation | async-start | bytes 9437184 | tf_op jit(solution)/shard_map/all_gather | solution.py:44
  8.2 2.0 copy-start.2
  9.6 249.2 %all-gather.5.cloned.1.call-start = ((), (), s32[]{:S(2)}) async-start(), calls=%async_computation.1 | async-start | bytes 9437184 | tf_op jit(solution)/shard_map/all_gather | solution.py:44
  10.6 8.0 %collective-permute-start.1 = (f32[512,2,128]{2,0,1:T(8,128)S(1)}, f32[512,2,128]{2,0,1:T(8,128)S(1)}, u32[]{:S(2)}, u32[]{:S(2)}) collective-permute-start(f32[512,2,128]{2,0,1:T(8,128)S(1)} %copy.44), channel_id=1, source_target_pairs={{1,0},{2,1},{3,2},{4,3},{5,4},{6,5},{7,6},{8,7},{9,8},{10,9},{11,1... | collective-permute-start | bytes 1572872 | tf_op jit(solution)/shard_map/ppermute | solution.py:18
  12.7 5.8 %copy-start.9 = (s32[8,128]{1,0:T(8,128)S(1)}, s32[8,128]{1,0:T(8,128)}, u32[]{:S(2)}) copy-start(s32[8,128]{1,0:T(8,128)} %param.9) | copy-start | bytes 12292
  12.7 5.8 %copy-start.8 = (f32[2,512]{1,0:T(2,128)S(1)}, f32[2,512]{1,0:T(2,128)}, u32[]{:S(2)}) copy-start(f32[2,512]{1,0:T(2,128)} %param.6) | copy-start | bytes 12292
  12.7 6.8 %collective-permute-start = (f32[512,2,128]{2,0,1:T(8,128)}, f32[512,2,128]{2,0,1:T(8,128)}, u32[]{:S(2)}, u32[]{:S(2)}) collective-permute-start(f32[512,2,128]{2,0,1:T(8,128)} %copy.43), channel_id=1, source_target_pairs={{0,1},{1,2},{2,3},{3,4},{4,5},{5,6},{6,7},{7,8},{8,9},{9,10},{10,1... | collective-permute-start | bytes 1572872 | tf_op jit(solution)/shard_map/ppermute | solution.py:15
  24.4 114.5 %copy-start.7 = (f32[512]{0:T(512)S(1)}, f32[512]{0:T(512)}, u32[]{:S(2)}) copy-start(f32[512]{0:T(512)} %param.7) | copy-start | bytes 6148
  122.4 16.5 %copy-start.1 = (f32[512,8,128]{0,2,1:T(8,128)S(1)}, f32[512,8,128]{0,2,1:T(8,128)}, u32[]{:S(2)}) copy-start(f32[512,8,128]{0,2,1:T(8,128)} %copy.31) | copy-start | bytes 6291460
  122.4 16.5 %copy-start.4 = (f32[512,2,128]{0,2,1:T(8,128)S(1)}, f32[512,2,128]{0,2,1:T(8,128)}, u32[]{:S(2)}) copy-start(f32[512,2,128]{0,2,1:T(8,128)} %copy.27) | copy-start | bytes 1572868
  122.4 16.5 %copy-start.6 = (f32[512,2,128]{0,2,1:T(8,128)S(1)}, f32[512,2,128]{0,2,1:T(8,128)}, u32[]{:S(2)}) copy-start(f32[512,2,128]{0,2,1:T(8,128)} %copy.22) | copy-start | bytes 1572868
  144.4 4.8 %collective-permute-start.3 = (f32[512,2,128]{2,0,1:T(8,128)S(1)}, f32[512,2,128]{2,0,1:T(8,128)S(1)}, u32[]{:S(2)}, u32[]{:S(2)}) collective-permute-start(f32[512,2,128]{2,0,1:T(8,128)S(1)} %copy.37), channel_id=1, source_target_pairs={{1,0},{2,1},{3,2},{4,3},{5,4},{6,5},{7,6},{8,7},{9,8},{10,9},{11,1... | collective-permute-start | bytes 1572872 | tf_op jit(solution)/shard_map/ppermute | solution.py:18
  145.9 4.6 %collective-permute-start.2 = (f32[512,2,128]{2,0,1:T(8,128)S(1)}, f32[512,2,128]{2,0,1:T(8,128)S(1)}, u32[]{:S(2)}, u32[]{:S(2)}) collective-permute-start(f32[512,2,128]{2,0,1:T(8,128)S(1)} %copy.35), channel_id=1, source_target_pairs={{0,1},{1,2},{2,3},{3,4},{4,5},{5,6},{6,7},{7,8},{8,9},{9,10},{10,1... | collective-permute-start | bytes 1572872 | tf_op jit(solution)/shard_map/ppermute | solution.py:15
  258.8 16.6 %copy-start = (f32[512,8,128]{0,2,1:T(8,128)S(1)}, f32[512,8,128]{0,2,1:T(8,128)}, u32[]{:S(2)}) copy-start(f32[512,8,128]{0,2,1:T(8,128)} %get-tuple-element.6) | copy-start | bytes 6291460
  258.8 16.6 %copy-start.3 = (f32[512,2,128]{0,2,1:T(8,128)S(1)}, f32[512,2,128]{0,2,1:T(8,128)}, u32[]{:S(2)}) copy-start(f32[512,2,128]{0,2,1:T(8,128)} %copy.38) | copy-start | bytes 1572868
  258.8 16.6 %copy-start.5 = (f32[512,2,128]{0,2,1:T(8,128)S(1)}, f32[512,2,128]{0,2,1:T(8,128)}, u32[]{:S(2)}) copy-start(f32[512,2,128]{0,2,1:T(8,128)} %copy.36) | copy-start | bytes 1572868
Sparse Core Ops, SparseCore 0:
  9.7 112.6 all-gather.2
  143.0 115.6 all-gather.4
where the time goes:
time: 289 us
  waiting for transfers between devices  203 us (70%)
  matrix products  33 us (11%)
  other arithmetic  14.6 us (5%)
  local copies, waits for them, and re-layouts  14.6 us (5%)
  between operations  13.6 us (5%)
  starting transfers between devices  9.82 us (3%)
    all_gather x2, waiting for transfers between devices, collide(): lax.all_gather(flat, 'mode', axis=0, tiled=True).astype(jnp.float32)  203 us
    dot_general x1, matrix products, collide(): jnp.dot(scatter_weight, lax.all_gather(flat, 'mode', axis=0, tiled=True)....  16.6 us
    reshape x1, matrix products, collide(): return gain.reshape(field.shape)  16.5 us
    ppermute x2, starting transfers between devices, extended(): lax.ppermute(lax.slice_in_dim(block, block.shape[dim] - width, None, axis...  7.19 us
  transfers between devices with their start and end apart: 6, of which 3 were waited for; matrix products, arithmetic and copies ran while one was open for 5% of the time, Pallas kernels for 0%

commit v1 on v0

v1 whole, which is shorter than its diff:
```python
import jax
import jax.numpy as jnp
from jax import lax
from jax.experimental import pallas as pl
from jax.experimental.pallas import tpu as pltpu
from jax.sharding import PartitionSpec as P

MESH = pl.DeviceIdType.MESH
f32 = jnp.float32
bf16 = jnp.bfloat16
MB = 512
NC = 128
ROWS = 8
NMODES = 4096
STAGE = 128
WU = 4
WR = 16
TOP = 31000.0


def kernel(dist, courant, rate, flags, weight, out,
           X, Fs, G, Cs, Cr, B, Wb, Wlo, Wst, Wsf, Wsh, coef, acc, wall, D,
           lsem, sx, rx, sz, rz, sf, rf, sc, rc, sh, rh,
           swx, rwx, swy, rwy, swf, rwf, swp, rwp):
    mi = lax.axis_index("mode")
    ti = lax.axis_index("tile")
    h, z = mi // 4, mi % 4
    y, l, c = ti // 4, (ti // 2) % 2, ti % 2

    def dev(h_, z_, y_, l_, c_):
        return (h_ * 4 + z_, y_ * 4 + l_ * 2 + c_)

    zp, zm, zz = (z + 1) % 4, (z + 3) % 4, (z + 2) % 4
    yp, ym, yy = (y + 1) % 4, (y + 3) % 4, (y + 2) % 4
    Ns = dev(h, z, y, 1 - l, c)
    No = dev(1 - h, z, y, 1 - l, c)
    Zp, Zm = dev(h, zp, y, l, c), dev(h, zm, y, l, c)
    Yp, Ym = dev(h, z, yp, l, c), dev(h, z, ym, l, c)
    Pc = dev(h, z, y, l, 1 - c)
    Hn, Hp = (mi, (ti + 1) % 16), (mi, (ti + 15) % 16)
    side = 1 - (h + l) % 2
    half_of = (1 - side, side)
    nbr = (Ns, No)
    hof = (h, 1 - h)
    q = y * 2 + c

    def row(half, j):
        return 3 - j + half * (1 + 2 * j)

    def rcopy(src, dst, ssem, rsem, to):
        return pltpu.make_async_remote_copy(
            src_ref=src, dst_ref=dst, send_sem=ssem, recv_sem=rsem,
            device_id=to, device_id_type=MESH)

    def cx(t, j, k):
        n = t * 4 + j
        return rcopy(Fs.at[t, row(half_of[k], j)], G.at[n, h * 4 + z],
                     sx.at[n, k], rx.at[n, k], nbr[k])

    def cx_in(n, k):
        blk = G.at[n, hof[k] * 4 + z]
        return rcopy(blk, blk, sx.at[n, k], rx.at[n, k], nbr[k])

    def cz(n, k, way):
        blk = G.at[n, hof[k] * 4 + z]
        return rcopy(blk, blk, sz.at[n, k, way], rz.at[n, k, way], (Zp, Zm)[way])

    def cz_in(n, k, way):
        blk = G.at[n, hof[k] * 4 + (zm, zp)[way]]
        return rcopy(blk, blk, sz.at[n, k, way], rz.at[n, k, way], (Zp, Zm)[way])

    def cf(n, way):
        blk = G.at[n, hof[way] * 4 + (zm, zp)[way]]
        return rcopy(blk, blk, sf.at[n, way], rf.at[n, way], (Zp, Zm)[way])

    def cf_in(n, way):
        blk = G.at[n, hof[way] * 4 + zz]
        return rcopy(blk, blk, sf.at[n, way], rf.at[n, way], (Zp, Zm)[way])

    def cc(n, k):
        return rcopy(Cs.at[n, k], Cr.at[n, k], sc.at[n, k], rc.at[n, k], nbr[k])

    def ch(t, d, way):
        src, dst = ((8 + d, d), (3 - d, 11 - d))[way]
        return rcopy(X.at[t, src], X.at[t, dst], sh.at[t, d, way], rh.at[t, d, way], (Hn, Hp)[way])

    def wrow(y_, c_, u):
        return Wb.at[1, (y_ * 2 + c_) * WU + u]

    def cwx(u):
        return rcopy(Wsh.at[u], wrow(y, c, u), swx.at[u], rwx.at[u], No)

    def cwy(u, way):
        blk = wrow(y, c, u)
        return rcopy(blk, blk, swy.at[u, way], rwy.at[u, way], (Yp, Ym)[way])

    def cwy_in(u, way):
        blk = wrow((ym, yp)[way], c, u)
        return rcopy(blk, blk, swy.at[u, way], rwy.at[u, way], (Yp, Ym)[way])

    def cwf(u):
        way = u % 2
        blk = wrow((ym, yp)[way], c, u)
        return rcopy(blk, blk, swf.at[u], rwf.at[u], (Yp, Ym)[way])

    def cwf_in(u):
        blk = wrow(yy, c, u)
        return rcopy(blk, blk, swf.at[u], rwf.at[u], (Yp, Ym)[u % 2])

    def cwp(y_, u):
        blk = wrow(y_, c, u)
        return rcopy(blk, blk, swp.at[y_, u], rwp.at[y_, u], Pc)

    def cwp_in(y_, u):
        blk = wrow(y_, 1 - c, u)
        return rcopy(blk, blk, swp.at[y_, u], rwp.at[y_, u], Pc)

    load_d = pltpu.make_async_copy(dist, D, lsem.at[0])
    load_s = pltpu.make_async_copy(weight.at[pl.ds(q * 64, 64)], Wsf, lsem.at[1])
    load_d.start()
    load_s.start()

    def load_w(i):
        return pltpu.make_async_copy(
            weight.at[pl.ds(i * STAGE, STAGE)], Wst.at[i % 2], lsem.at[2 + i % 2])

    load_w(0).start()
    load_w(1).start()

    barrier = pltpu.get_barrier_semaphore()
    for to in (Ns, No, Zp, Zm, Yp, Ym, Pc, Hn, Hp):
        pl.semaphore_signal(barrier, inc=1, device_id=to, device_id_type=MESH)
    pl.semaphore_wait(barrier, 9)

    load_d.wait()

    def take(r):
        v = D[pl.ds(r, MB, stride=ROWS), :]
        X[0, 2 + r] = v
        Fs[0, r] = v.astype(bf16)

    def first_send(j):
        take(3 - j)
        take(4 + j)
        cx(0, j, 0).start()
        cx(0, j, 1).start()

    shared = []

    def share(u):
        if not shared:
            load_s.wait()
        shared.append(u)
        Wsh[u] = Wsf[pl.ds(u * WR, WR), :].astype(bf16)
        cwx(u).start()

    def halo(t, d):
        ch(t, d, 0).start()
        ch(t, d, 1).start()

    def zown(n, k):
        cx_in(n, k).wait_recv()
        cz(n, k, 0).start()
        cz(n, k, 1).start()

    def zfwd(n, k):
        cz_in(n, k, k).wait_recv()
        cf(n, k).start()

    def cast_w(i):
        load_w(i).wait()

        @pl.loop(0, STAGE // WR)
        def _(r):
            v = Wst[i % 2, pl.ds(r * WR, WR), :]
            high_part = v.astype(bf16)
            Wb[0, i * (STAGE // WR) + r] = high_part
            Wlo[i * (STAGE // WR) + r] = (v - high_part.astype(f32)).astype(bf16)

        if i + 2 < MB // STAGE:
            load_w(i + 2).start()

    def w1(u):
        cwx(u).wait_recv()
        cwy(u, 0).start()
        cwy(u, 1).start()
        cwp(y, u).start()

    def w2(u, way):
        cwy_in(u, way).wait_recv()
        if u % 2 == way:
            cwf(u).start()
        cwp((ym, yp)[way], u).start()

    def w3(u):
        cwf_in(u).wait_recv()
        cwp(yy, u).start()

    def wfin():
        for u in range(WU):
            for y_ in (y, ym, yp, yy):
                cwp_in(y_, u).wait_recv()

    def coefs():
        for r in range(ROWS):
            wall[r] = jnp.broadcast_to(0.5 * flags[r:r + 1, :].astype(f32), (8, NC))
        for i in range(MB // NC):
            at = pl.ds(i * NC, NC)
            for k, line in ((0, courant[0:1, at]), (1, courant[1:2, at]), (2, rate[0:1, at])):
                coef[k, at, :] = jnp.transpose(jnp.broadcast_to(line, (NC, NC)))

    low = jnp.where(ti > 0, 1.0, 0.0).astype(f32)
    high = jnp.where(ti < 15, 1.0, 0.0).astype(f32)

    def base(t, edge):
        if edge:
            for d in (0, 1):
                ch(t, d, 0).wait_recv()
                ch(t, d, 1).wait_recv()
        rows = (0, 1, 6, 7) if edge else (2, 3, 4, 5)
        used = sorted({r + d for r in rows for d in range(5)})
        lane = lax.broadcasted_iota(jnp.int32, (8, NC), 1)

        def modes(g):
            at = pl.ds(pl.multiple_of(g * 8, 8), 8)
            vx, vy, rt = coef[0, at, :], coef[1, at, :], coef[2, at, :]
            px, nx = jnp.maximum(vx, 0.0), jnp.minimum(vx, 0.0)
            py, ny = jnp.maximum(vy, 0.0), jnp.minimum(vy, 0.0)
            diag = 1.0 - 1.5 * ((px - nx) + (py - ny)) - 0.25 * rt
            a1, a2, b1, b2 = 2.0 * px, -0.5 * px, -2.0 * nx, 0.5 * nx
            e1 = jnp.where(lane >= 1, 2.0 * py, 0.0)
            e2 = jnp.where(lane >= 2, -0.5 * py, 0.0)
            g1 = jnp.where(lane < NC - 1, -2.0 * ny, 0.0)
            g2 = jnp.where(lane < NC - 2, 0.5 * ny, 0.0)
            x = {r: X[t, r, at, :] for r in used}
            if edge:
                x[0], x[1] = x[0] * low, x[1] * low
                x[10], x[11] = x[10] * high, x[11] * high
            for r in rows:
                f = x[r + 2]
                v = f * (diag - wall[r])
                v = v + a1 * x[r + 1] + a2 * x[r] + b1 * x[r + 3] + b2 * x[r + 4]
                v = v + e1 * pltpu.roll(f, 1, 1) + e2 * pltpu.roll(f, 2, 1)
                v = v + g1 * pltpu.roll(f, NC - 1, 1) + g2 * pltpu.roll(f, NC - 2, 1)
                B[r, at, :] = v

        @pl.loop(0, MB // 32)
        def _(g):
            for i in range(4):
                modes(g * 4 + i)

    def ship(n, k, v):
        top = jnp.maximum(jnp.max(jnp.abs(v), axis=0, keepdims=True), 1e-20)
        power = jnp.ceil(jnp.log2(top))
        code = jnp.round(v * (jnp.exp2(-power) * TOP))
        Cs[n, k, 0:MB, :] = code.astype(jnp.int32).astype(jnp.int16)
        Cs[n, k, MB:MB + 16, :] = jnp.broadcast_to(power, (16, NC)).astype(jnp.int32).astype(jnp.int16)
        cc(n, k).start()

    def quarter(n, k):
        power = Cr[n, k, MB:MB + 16, :].astype(jnp.int32).astype(f32)[0:1, :]
        return Cr[n, k, 0:MB, :].astype(jnp.int32).astype(f32) * (jnp.exp2(power) * (0.25 / TOP))

    parts = (lambda at: (Wb[0, :, :, at], Wlo[:, :, at]), lambda at: (Wb[1, :, :, at],))

    def times(w, at, g):
        total = None
        for part in parts[w](at):
            term = jnp.dot(part.reshape(MB, -1), g, preferred_element_type=f32)
            total = term if total is None else total + term
        return total

    def gain(w, *ns):
        if w == 0:
            for n in ns:
                for k in (0, 1):
                    cz_in(n, k, 1 - k).wait_recv()
                    cf_in(n, k).wait_recv()
        cells = [G[n].reshape(NMODES, NC) for n in ns]
        cells = cells[0] if len(ns) == 1 else jnp.concatenate(cells, axis=1)
        acc[:, 0:len(ns) * NC] = times(w, slice(None), cells)
        for i, n in enumerate(ns):
            ship(n, w, acc[:, i * NC:(i + 1) * NC])

    def layer(w, n, z_):
        at = [pl.ds(pl.multiple_of(hh * 4 * MB + z_ * MB, MB), MB) for hh in (0, 1)]
        cells = [G[n, z_], G[n, 4 + z_]]
        terms = list(zip(*(parts[w](a) for a in at)))
        left = [v.reshape(MB, MB) for term in terms for v in term]
        return jnp.dot(jnp.concatenate(left, axis=1), jnp.concatenate(cells * len(terms), axis=0),
                       preferred_element_type=f32)

    def early(n):
        cz_in(n, 0, 1).wait_recv()
        cz_in(n, 1, 0).wait_recv()
        for w in (0, 1):
            at = pl.ds(w * NC, NC)
            acc[:, at] = layer(w, n, z)

            @pl.loop(0, 2)
            def _(i):
                acc[:, at] += layer(w, n, (z + 1 + 2 * i) % 4)

    def late(n, w):
        if w == 0:
            cf_in(n, 0).wait_recv()
            cf_in(n, 1).wait_recv()
        ship(n, w, acc[:, w * NC:(w + 1) * NC] + layer(w, n, zz))

    def u1(j, k):
        cc(j, k).wait_recv()
        r = row(half_of[k], j)
        v = B[r] + quarter(j, k)
        X[1, 2 + r] = v
        Fs[1, r] = v.astype(bf16)
        cx(1, j, k).start()

    def u2(j):
        n = 4 + j
        cc(n, 0).wait_recv()
        cc(n, 1).wait_recv()
        at0 = half_of[0]
        D[pl.ds(3 - j, MB, stride=ROWS), :] = B[3 - j] + quarter(n, at0)
        D[pl.ds(4 + j, MB, stride=ROWS), :] = B[4 + j] + quarter(n, 1 - at0)

    share(1)
    share(2)
    first_send(0)
    cast_w(0)
    first_send(1)
    cast_w(1)
    share(0)
    share(3)
    w1(1)
    zown(0, 0)
    w1(2)
    first_send(2)
    zown(1, 0)
    coefs()
    first_send(3)
    cast_w(2)
    zown(0, 1)
    halo(0, 0)
    w2(1, 1)
    w2(2, 0)
    zown(1, 1)
    zfwd(0, 0)
    cast_w(3)
    w1(0)
    zfwd(1, 0)
    zfwd(0, 1)
    w1(3)
    zfwd(1, 1)
    w2(2, 1)
    w2(0, 1)
    w3(1)
    zown(2, 0)
    zown(3, 0)
    w2(0, 0)
    base(0, 0)
    w2(3, 0)
    w2(3, 1)
    gain(0, 0, 1)
    w3(0)
    zown(3, 1)
    w3(2)
    zfwd(2, 0)
    w2(1, 0)
    zown(2, 1)
    w3(3)
    wfin()
    gain(1, 0, 1)
    zfwd(3, 0)
    zfwd(3, 1)
    u1(0, 0)
    u1(1, 0)
    zfwd(2, 1)
    halo(0, 1)
    zown(4, 0)
    u1(0, 1)
    u1(1, 1)
    zown(5, 0)
    gain(0, 2, 3)
    zown(4, 1)
    gain(1, 2, 3)
    zown(5, 1)
    zfwd(5, 0)
    base(0, 1)
    zfwd(4, 1)
    zfwd(4, 0)
    u1(2, 0)
    zfwd(5, 1)
    u1(2, 1)
    u1(3, 0)
    zown(6, 0)
    zown(6, 1)
    u1(3, 1)
    halo(1, 1)
    zown(7, 0)
    gain(0, 4, 5)
    halo(1, 0)
    zfwd(6, 1)
    zfwd(6, 0)
    gain(1, 4, 5)
    zown(7, 1)
    zfwd(7, 0)
    base(1, 0)
    gain(0, 6)
    zfwd(7, 1)
    gain(1, 6)
    early(7)
    late(7, 0)
    late(7, 1)
    u2(1)
    base(1, 1)
    u2(0)
    u2(2)
    u2(3)
    store = pltpu.make_async_copy(D, out, lsem.at[0])
    store.start()

    for t in (0, 1):
        for k in (0, 1):
            ch(t, 0, k).wait_send()
            ch(t, 1, k).wait_send()
        for j in range(4):
            for k in (0, 1):
                cx(t, j, k).wait_send()
    for n in range(8):
        for k in (0, 1):
            cz(n, 0, k).wait_send()
            cz(n, 1, k).wait_send()
            cf(n, k).wait_send()
            cc(n, k).wait_send()
    for u in range(WU):
        cwx(u).wait_send()
        cwy(u, 0).wait_send()
        cwy(u, 1).wait_send()
        cwf(u).wait_send()
        for y_ in range(4):
            cwp(y_, u).wait_send()
    store.wait()


def body(distribution, courant, relax_rate, scatter_weight, cell_flags):
    vmem = pl.BlockSpec(memory_space=pltpu.VMEM)
    hbm = pl.BlockSpec(memory_space=pl.ANY)
    dma = pltpu.SemaphoreType.DMA
    out = pl.pallas_call(
        kernel,
        out_shape=jax.ShapeDtypeStruct((MB * ROWS, NC), f32),
        in_specs=[hbm, vmem, vmem, vmem, hbm],
        out_specs=hbm,
        scratch_shapes=[
            pltpu.VMEM((2, 12, MB, NC), f32),
            pltpu.VMEM((2, ROWS, MB, NC), bf16),
            pltpu.VMEM((8, 8, MB, NC), bf16),
            pltpu.VMEM((8, 2, MB + 16, NC), jnp.int16),
            pltpu.VMEM((8, 2, MB + 16, NC), jnp.int16),
            pltpu.VMEM((ROWS, MB, NC), f32),
            pltpu.VMEM((2, MB // WR, WR, NMODES), bf16),
            pltpu.VMEM((MB // WR, WR, NMODES), bf16),
            pltpu.VMEM((2, STAGE, NMODES), f32),
            pltpu.VMEM((64, NMODES), f32),
            pltpu.VMEM((WU, WR, NMODES), bf16),
            pltpu.VMEM((3, MB, NC), f32),
            pltpu.VMEM((MB, 2 * NC), f32),
            pltpu.VMEM((ROWS, 8, NC), f32),
            pltpu.VMEM((MB * ROWS, NC), f32),
            dma((4,)),
            dma((8, 2)), dma((8, 2)),
            dma((8, 2, 2)), dma((8, 2, 2)),
            dma((8, 2)), dma((8, 2)),
            dma((8, 2)), dma((8, 2)),
            dma((2, 2, 2)), dma((2, 2, 2)),
            dma((WU,)), dma((WU,)),
            dma((WU, 2)), dma((WU, 2)),
            dma((WU,)), dma((WU,)),
            dma((4, WU)), dma((4, WU)),
        ],
        compiler_params=pltpu.CompilerParams(
            collective_id=0, has_side_effects=True, vmem_limit_bytes=60 * 1024 * 1024),
    )(distribution.reshape(MB * ROWS, NC), courant, relax_rate.reshape(1, MB),
      cell_flags, scatter_weight)
    return out.reshape(distribution.shape)


def solution(mesh):
    in_specs = (
        P("mode", "tile", None),
        P(None, "mode"),
        P("mode"),
        P("mode", None),
        P("tile", None),
    )
    out_specs = P("mode", "tile", None)
    return jax.shard_map(body, mesh=mesh, in_specs=in_specs, out_specs=out_specs, check_vma=False)
```

time: 289 us -> 104 us (0.36)
  waiting for transfers between devices: 203 us -> 0 us
  Pallas kernels: 0 us -> 101 us
  matrix products: 33 us -> 0 us
  other arithmetic: 14.6 us -> 0 us
  between operations: 13.6 us -> 0.01 us
  local copies, waits for them, and re-layouts: 14.6 us -> 3.05 us
  starting transfers between devices: 9.82 us -> 0 us
    all_gather x2 -> x0, waiting for transfers between devices: 203 us -> none  [collide(): lax.all_gather(flat, 'mode', axis=0, tiled=True).astype(jnp.float32)]
    pallas_call x0 -> x1, Pallas kernels: none -> 101 us  [body(): pl.pallas_call(kernel, out_shape=jax.ShapeDtypeStruct((MB * ROWS, NC), f3...]
    dot_general x1 -> x0, matrix products: 16.6 us -> none  [collide(): jnp.dot(scatter_weight, lax.all_gather(flat, 'mode', axis=0, tiled=True)....]
    reshape x1 -> x0, matrix products: 16.5 us -> none  [collide(): return gain.reshape(field.shape)]
    ppermute x4 -> x0, starting transfers between devices: 9.78 us -> none  [the longest x2 7.19 us: extended(): lax.ppermute(lax.slice_in_dim(block, block.shape[dim] - width, None, axis...]
    convert_element_type x2 -> x0, other arithmetic: 5.63 us -> none  [collide(): rounded = field.astype(jnp.bfloat16)]
    concatenate x2 -> x0, other arithmetic: 5.25 us -> none  [extended(): block = jnp.concatenate([low, block, high], axis=dim)]
    ppermute x4 -> x0, local copies, waits for them, and re-layouts: 5.1 us -> none  [the longest x2 3.1 us: extended(): lax.ppermute(lax.slice_in_dim(block, block.shape[dim] - width, None, axis...]
  transfers between devices with their start and end apart: 6 -> 0, of which waited for: 3 -> 0; matrix products, arithmetic and copies ran while one was open for 5% -> 0% of each run, Pallas kernels for 0% -> 0%
where the time goes in v1:
time: 104 us
  Pallas kernels  101 us (97%)
  local copies, waits for them, and re-layouts  3.05 us (3%)
    pallas_call x1, Pallas kernels, body(): pl.pallas_call(kernel, out_shape=jax.ShapeDtypeStruct((MB * ROWS, NC), f3...  101 us
    unnamed x1, local copies, waits for them, and re-layouts  3.05 us

profile of v1, /device:TPU:0, one launch (start us, length us, event | category | flops | bytes accessed | tf_op | source)
XLA Modules:
  0.0 104.1 jit_solution(15814261259155810161)
XLA Ops:
  0.0 101.0 %shard_map.55 = f32[4096,128]{1,0:T(8,128)} custom-call(f32[4096,128]{1,0:T(8,128)} %bitcast.4, f32[2,512]{1,0:T(2,128)} %courant.1, f32[1,512]{1,0:T(1,128)} %bitcast.5, s32[8,128]{1,0:T(8,128)} %flags.1, f32[512,4096]{1,0:T(8,128)} %weight.1), custom_call_target="tpu_custom_call" | custom-call | tf_op jit(solution)/shard_map/pallas_call | solution.py:449
  101.0 3.0 %copy.7 = f32[512,8,128]{2,1,0:T(8,128)} copy(f32[512,8,128]{2,1,0:T(8,128)} %bitcast.3) | data formatting | bytes 4194304

commit v2 on v1

--- a/solution.py
+++ b/solution.py
@@ -130,8 +130,6 @@
     barrier = pltpu.get_barrier_semaphore()
     for to in (Ns, No, Zp, Zm, Yp, Ym, Pc, Hn, Hp):
         pl.semaphore_signal(barrier, inc=1, device_id=to, device_id_type=MESH)
-    pl.semaphore_wait(barrier, 9)
-
     load_d.wait()
 
     def take(r):
@@ -140,33 +138,21 @@
         Fs[0, r] = v.astype(bf16)
 
     def first_send(j):
-        take(3 - j)
-        take(4 + j)
         cx(0, j, 0).start()
         cx(0, j, 1).start()
 
-    shared = []
-
     def share(u):
-        if not shared:
-            load_s.wait()
-        shared.append(u)
-        Wsh[u] = Wsf[pl.ds(u * WR, WR), :].astype(bf16)
         cwx(u).start()
 
     def halo(t, d):
         ch(t, d, 0).start()
         ch(t, d, 1).start()
 
-    def zown(n, k):
-        cx_in(n, k).wait_recv()
-        cz(n, k, 0).start()
-        cz(n, k, 1).start()
-
-    def zfwd(n, k):
-        cz_in(n, k, k).wait_recv()
-        cf(n, k).start()
-
+    for r in (3, 4, 2, 5, 1, 6, 0, 7):
+        take(r)
+    load_s.wait()
+    for u in range(WU):
+        Wsh[u] = Wsf[pl.ds(u * WR, WR), :].astype(bf16)
     def cast_w(i):
         load_w(i).wait()
 
@@ -180,6 +166,39 @@
         if i + 2 < MB // STAGE:
             load_w(i + 2).start()
 
+    def coefs():
+        for r in range(ROWS):
+            wall[r] = jnp.broadcast_to(0.5 * flags[r:r + 1, :].astype(f32), (8, NC))
+        for i in range(MB // NC):
+            at = pl.ds(i * NC, NC)
+            vx, vy, rt = (jnp.transpose(jnp.broadcast_to(line, (NC, NC)))
+                          for line in (courant[0:1, at], courant[1:2, at], rate[0:1, at]))
+            lane = lax.broadcasted_iota(jnp.int32, (NC, NC), 1)
+            ax = jnp.abs(vx)
+            py, ny = jnp.maximum(vy, 0.0), jnp.minimum(vy, 0.0)
+            coef[0, at, :] = vx
+            coef[1, at, :] = 1.0 - 1.5 * (ax + jnp.abs(vy)) - 0.25 * rt
+            coef[2, at, :] = 2.0 * ax
+            coef[3, at, :] = -0.5 * ax
+            coef[4, at, :] = jnp.where(lane >= 1, 2.0 * py, 0.0)
+            coef[5, at, :] = jnp.where(lane >= 2, -0.5 * py, 0.0)
+            coef[6, at, :] = jnp.where(lane < NC - 1, -2.0 * ny, 0.0)
+            coef[7, at, :] = jnp.where(lane < NC - 2, 0.5 * ny, 0.0)
+
+    for i in range(MB // STAGE):
+        cast_w(i)
+    coefs()
+    pl.semaphore_wait(barrier, 9)
+
+    def zown(n, k):
+        cx_in(n, k).wait_recv()
+        cz(n, k, 0).start()
+        cz(n, k, 1).start()
+
+    def zfwd(n, k):
+        cz_in(n, k, k).wait_recv()
+        cf(n, k).start()
+
     def w1(u):
         cwx(u).wait_recv()
         cwy(u, 0).start()
@@ -200,14 +219,6 @@
         for u in range(WU):
             for y_ in (y, ym, yp, yy):
                 cwp_in(y_, u).wait_recv()
-
-    def coefs():
-        for r in range(ROWS):
-            wall[r] = jnp.broadcast_to(0.5 * flags[r:r + 1, :].astype(f32), (8, NC))
-        for i in range(MB // NC):
-            at = pl.ds(i * NC, NC)
-            for k, line in ((0, courant[0:1, at]), (1, courant[1:2, at]), (2, rate[0:1, at])):
-                coef[k, at, :] = jnp.transpose(jnp.broadcast_to(line, (NC, NC)))
 
     low = jnp.where(ti > 0, 1.0, 0.0).astype(f32)
     high = jnp.where(ti < 15, 1.0, 0.0).astype(f32)
@@ -219,19 +230,11 @@
                 ch(t, d, 1).wait_recv()
         rows = (0, 1, 6, 7) if edge else (2, 3, 4, 5)
         used = sorted({r + d for r in rows for d in range(5)})
-        lane = lax.broadcasted_iota(jnp.int32, (8, NC), 1)
 
         def modes(g):
             at = pl.ds(pl.multiple_of(g * 8, 8), 8)
-            vx, vy, rt = coef[0, at, :], coef[1, at, :], coef[2, at, :]
-            px, nx = jnp.maximum(vx, 0.0), jnp.minimum(vx, 0.0)
-            py, ny = jnp.maximum(vy, 0.0), jnp.minimum(vy, 0.0)
-            diag = 1.0 - 1.5 * ((px - nx) + (py - ny)) - 0.25 * rt
-            a1, a2, b1, b2 = 2.0 * px, -0.5 * px, -2.0 * nx, 0.5 * nx
-            e1 = jnp.where(lane >= 1, 2.0 * py, 0.0)
-            e2 = jnp.where(lane >= 2, -0.5 * py, 0.0)
-            g1 = jnp.where(lane < NC - 1, -2.0 * ny, 0.0)
-            g2 = jnp.where(lane < NC - 2, 0.5 * ny, 0.0)
+            vx, diag, a1, a2, e1, e2, g1, g2 = (coef[i, at, :] for i in range(8))
+            up = vx > 0.0
             x = {r: X[t, r, at, :] for r in used}
             if edge:
                 x[0], x[1] = x[0] * low, x[1] * low
@@ -239,15 +242,15 @@
             for r in rows:
                 f = x[r + 2]
                 v = f * (diag - wall[r])
-                v = v + a1 * x[r + 1] + a2 * x[r] + b1 * x[r + 3] + b2 * x[r + 4]
+                v = v + a1 * jnp.where(up, x[r + 1], x[r + 3]) + a2 * jnp.where(up, x[r], x[r + 4])
                 v = v + e1 * pltpu.roll(f, 1, 1) + e2 * pltpu.roll(f, 2, 1)
                 v = v + g1 * pltpu.roll(f, NC - 1, 1) + g2 * pltpu.roll(f, NC - 2, 1)
                 B[r, at, :] = v
 
-        @pl.loop(0, MB // 32)
+        @pl.loop(0, MB // 64)
         def _(g):
-            for i in range(4):
-                modes(g * 4 + i)
+            for i in range(8):
+                modes(g * 8 + i)
 
     def ship(n, k, v):
         top = jnp.maximum(jnp.max(jnp.abs(v), axis=0, keepdims=True), 1e-20)
@@ -324,87 +327,82 @@
         D[pl.ds(4 + j, MB, stride=ROWS), :] = B[4 + j] + quarter(n, 1 - at0)
 
     share(1)
+    share(0)
+    first_send(0)
+    first_send(1)
+    share(3)
     share(2)
-    first_send(0)
-    cast_w(0)
-    first_send(1)
-    cast_w(1)
-    share(0)
-    share(3)
     w1(1)
     zown(0, 0)
-    w1(2)
     first_send(2)
     zown(1, 0)
-    coefs()
+    w1(0)
     first_send(3)
-    cast_w(2)
     zown(0, 1)
     halo(0, 0)
-    w2(1, 1)
-    w2(2, 0)
     zown(1, 1)
     zfwd(0, 0)
-    cast_w(3)
-    w1(0)
+    w2(1, 1)
+    w2(0, 0)
+    w1(3)
+    zfwd(0, 1)
     zfwd(1, 0)
-    zfwd(0, 1)
-    w1(3)
+    base(0, 0)
     zfwd(1, 1)
+    w1(2)
+    w2(3, 1)
+    w3(0)
+    w2(3, 0)
+    zown(3, 0)
+    zown(2, 1)
+    w3(1)
+    w2(2, 0)
+    w2(0, 1)
+    w2(1, 0)
+    gain(0, 0, 1)
     w2(2, 1)
-    w2(0, 1)
-    w3(1)
     zown(2, 0)
-    zown(3, 0)
-    w2(0, 0)
-    base(0, 0)
-    w2(3, 0)
-    w2(3, 1)
-    gain(0, 0, 1)
-    w3(0)
+    zfwd(3, 0)
     zown(3, 1)
+    w3(3)
     w3(2)
-    zfwd(2, 0)
-    w2(1, 0)
-    zown(2, 1)
-    w3(3)
+    zfwd(2, 1)
     wfin()
     gain(1, 0, 1)
-    zfwd(3, 0)
-    zfwd(3, 1)
     u1(0, 0)
     u1(1, 0)
-    zfwd(2, 1)
+    zfwd(3, 1)
+    zfwd(2, 0)
+    u1(0, 1)
+    zown(4, 0)
     halo(0, 1)
-    zown(4, 0)
-    u1(0, 1)
     u1(1, 1)
     zown(5, 0)
     gain(0, 2, 3)
     zown(4, 1)
     gain(1, 2, 3)
     zown(5, 1)
-    zfwd(5, 0)
     base(0, 1)
+    u1(2, 0)
     zfwd(4, 1)
     zfwd(4, 0)
-    u1(2, 0)
     zfwd(5, 1)
+    u1(3, 0)
+    zfwd(5, 0)
     u1(2, 1)
-    u1(3, 0)
+    u1(3, 1)
     zown(6, 0)
+    halo(1, 1)
+    base(1, 0)
     zown(6, 1)
-    u1(3, 1)
-    halo(1, 1)
     zown(7, 0)
     gain(0, 4, 5)
-    halo(1, 0)
     zfwd(6, 1)
     zfwd(6, 0)
     gain(1, 4, 5)
     zown(7, 1)
+    halo(1, 0)
     zfwd(7, 0)
-    base(1, 0)
     gain(0, 6)
     zfwd(7, 1)
     gain(1, 6)
@@ -413,8 +411,8 @@
     late(7, 1)
     u2(1)
     base(1, 1)
+    u2(2)
     u2(0)
-    u2(2)
     u2(3)
     store = pltpu.make_async_copy(D, out, lsem.at[0])
     store.start()
@@ -463,7 +461,7 @@
             pltpu.VMEM((2, STAGE, NMODES), f32),
             pltpu.VMEM((64, NMODES), f32),
             pltpu.VMEM((WU, WR, NMODES), bf16),
-            pltpu.VMEM((3, MB, NC), f32),
+            pltpu.VMEM((8, MB, NC), f32),
             pltpu.VMEM((MB, 2 * NC), f32),
             pltpu.VMEM((ROWS, 8, NC), f32),
             pltpu.VMEM((MB * ROWS, NC), f32),

time: 104 us -> 109 us (1.048)
  Pallas kernels: 101 us -> 105 us
    pallas_call x1, Pallas kernels: 101 us -> 105 us  [body(): pl.pallas_call(kernel, out_shape=jax.ShapeDtypeStruct((MB * ROWS, NC), f3...]
where the time goes in v2:
time: 109 us; the launch traced here: 108 us
  Pallas kernels  105 us (96%)
  local copies, waits for them, and re-layouts  3.05 us (3%)
    pallas_call x1, Pallas kernels, body(): pl.pallas_call(kernel, out_shape=jax.ShapeDtypeStruct((MB * ROWS, NC), f3...  105 us
    unnamed x1, local copies, waits for them, and re-layouts  3.05 us

profile of v2, /device:TPU:0, one launch (start us, length us, event | category | flops | bytes accessed | tf_op | source)
XLA Modules:
  0.0 108.4 jit_solution(7460064157663015894)
XLA Ops:
  0.0 105.3 %shard_map.55 = f32[4096,128]{1,0:T(8,128)} custom-call(f32[4096,128]{1,0:T(8,128)} %bitcast.4, f32[2,512]{1,0:T(2,128)} %courant.1, f32[1,512]{1,0:T(1,128)} %bitcast.5, s32[8,128]{1,0:T(8,128)} %flags.1, f32[512,4096]{1,0:T(8,128)} %weight.1), custom_call_target="tpu_custom_call" | custom-call | tf_op jit(solution)/shard_map/pallas_call | solution.py:447
  105.3 3.0 %copy.7 = f32[512,8,128]{2,1,0:T(8,128)} copy(f32[512,8,128]{2,1,0:T(8,128)} %bitcast.3) | data formatting | bytes 4194304

commit v3 on v1

--- a/solution.py
+++ b/solution.py
@@ -19,7 +19,7 @@
 
 
 def kernel(dist, courant, rate, flags, weight, out,
-           X, Fs, G, Cs, Cr, B, Wb, Wlo, Wst, Wsf, Wsh, coef, acc, wall, D,
+           X, Fs, G, Cs, Cr, B, Wb, Wst, Wsf, Wsh, coef, acc, wall, D,
            lsem, sx, rx, sz, rz, sf, rf, sc, rc, sh, rh,
            swx, rwx, swy, rwy, swf, rwf, swp, rwp):
     mi = lax.axis_index("mode")
@@ -173,9 +173,7 @@
         @pl.loop(0, STAGE // WR)
         def _(r):
             v = Wst[i % 2, pl.ds(r * WR, WR), :]
-            high_part = v.astype(bf16)
-            Wb[0, i * (STAGE // WR) + r] = high_part
-            Wlo[i * (STAGE // WR) + r] = (v - high_part.astype(f32)).astype(bf16)
+            Wb[0, i * (STAGE // WR) + r] = v.astype(bf16)
 
         if i + 2 < MB // STAGE:
             load_w(i + 2).start()
@@ -206,8 +204,19 @@
             wall[r] = jnp.broadcast_to(0.5 * flags[r:r + 1, :].astype(f32), (8, NC))
         for i in range(MB // NC):
             at = pl.ds(i * NC, NC)
-            for k, line in ((0, courant[0:1, at]), (1, courant[1:2, at]), (2, rate[0:1, at])):
-                coef[k, at, :] = jnp.transpose(jnp.broadcast_to(line, (NC, NC)))
+            vx, vy, rt = (jnp.transpose(jnp.broadcast_to(line, (NC, NC)))
+                          for line in (courant[0:1, at], courant[1:2, at], rate[0:1, at]))
+            lane = lax.broadcasted_iota(jnp.int32, (NC, NC), 1)
+            ax = jnp.abs(vx)
+            py, ny = jnp.maximum(vy, 0.0), jnp.minimum(vy, 0.0)
+            coef[0, at, :] = vx
+            coef[1, at, :] = 1.0 - 1.5 * (ax + jnp.abs(vy)) - 0.25 * rt
+            coef[2, at, :] = 2.0 * ax
+            coef[3, at, :] = -0.5 * ax
+            coef[4, at, :] = jnp.where(lane >= 1, 2.0 * py, 0.0)
+            coef[5, at, :] = jnp.where(lane >= 2, -0.5 * py, 0.0)
+            coef[6, at, :] = jnp.where(lane < NC - 1, -2.0 * ny, 0.0)
+            coef[7, at, :] = jnp.where(lane < NC - 2, 0.5 * ny, 0.0)
 
     low = jnp.where(ti > 0, 1.0, 0.0).astype(f32)
     high = jnp.where(ti < 15, 1.0, 0.0).astype(f32)
@@ -219,19 +228,11 @@
                 ch(t, d, 1).wait_recv()
         rows = (0, 1, 6, 7) if edge else (2, 3, 4, 5)
         used = sorted({r + d for r in rows for d in range(5)})
-        lane = lax.broadcasted_iota(jnp.int32, (8, NC), 1)
 
         def modes(g):
             at = pl.ds(pl.multiple_of(g * 8, 8), 8)
-            vx, vy, rt = coef[0, at, :], coef[1, at, :], coef[2, at, :]
-            px, nx = jnp.maximum(vx, 0.0), jnp.minimum(vx, 0.0)
-            py, ny = jnp.maximum(vy, 0.0), jnp.minimum(vy, 0.0)
-            diag = 1.0 - 1.5 * ((px - nx) + (py - ny)) - 0.25 * rt
-            a1, a2, b1, b2 = 2.0 * px, -0.5 * px, -2.0 * nx, 0.5 * nx
-            e1 = jnp.where(lane >= 1, 2.0 * py, 0.0)
-            e2 = jnp.where(lane >= 2, -0.5 * py, 0.0)
-            g1 = jnp.where(lane < NC - 1, -2.0 * ny, 0.0)
-            g2 = jnp.where(lane < NC - 2, 0.5 * ny, 0.0)
+            vx, diag, a1, a2, e1, e2, g1, g2 = (coef[i, at, :] for i in range(8))
+            up = vx > 0.0
             x = {r: X[t, r, at, :] for r in used}
             if edge:
                 x[0], x[1] = x[0] * low, x[1] * low
@@ -239,15 +240,15 @@
             for r in rows:
                 f = x[r + 2]
                 v = f * (diag - wall[r])
-                v = v + a1 * x[r + 1] + a2 * x[r] + b1 * x[r + 3] + b2 * x[r + 4]
+                v = v + a1 * jnp.where(up, x[r + 1], x[r + 3]) + a2 * jnp.where(up, x[r], x[r + 4])
                 v = v + e1 * pltpu.roll(f, 1, 1) + e2 * pltpu.roll(f, 2, 1)
                 v = v + g1 * pltpu.roll(f, NC - 1, 1) + g2 * pltpu.roll(f, NC - 2, 1)
                 B[r, at, :] = v
 
-        @pl.loop(0, MB // 32)
+        @pl.loop(0, MB // 64)
         def _(g):
-            for i in range(4):
-                modes(g * 4 + i)
+            for i in range(8):
+                modes(g * 8 + i)
 
     def ship(n, k, v):
         top = jnp.maximum(jnp.max(jnp.abs(v), axis=0, keepdims=True), 1e-20)
@@ -261,7 +262,7 @@
         power = Cr[n, k, MB:MB + 16, :].astype(jnp.int32).astype(f32)[0:1, :]
         return Cr[n, k, 0:MB, :].astype(jnp.int32).astype(f32) * (jnp.exp2(power) * (0.25 / TOP))
 
-    parts = (lambda at: (Wb[0, :, :, at], Wlo[:, :, at]), lambda at: (Wb[1, :, :, at],))
+    parts = (lambda at: (Wb[0, :, :, at],), lambda at: (Wb[1, :, :, at],))
 
     def times(w, at, g):
         total = None
@@ -459,11 +460,10 @@
             pltpu.VMEM((8, 2, MB + 16, NC), jnp.int16),
             pltpu.VMEM((ROWS, MB, NC), f32),
             pltpu.VMEM((2, MB // WR, WR, NMODES), bf16),
-            pltpu.VMEM((MB // WR, WR, NMODES), bf16),
             pltpu.VMEM((2, STAGE, NMODES), f32),
             pltpu.VMEM((64, NMODES), f32),
             pltpu.VMEM((WU, WR, NMODES), bf16),
-            pltpu.VMEM((3, MB, NC), f32),
+            pltpu.VMEM((8, MB, NC), f32),
             pltpu.VMEM((MB, 2 * NC), f32),
             pltpu.VMEM((ROWS, 8, NC), f32),
             pltpu.VMEM((MB * ROWS, NC), f32),

time: 104 us -> 97.8 us (0.940)
  Pallas kernels: 101 us -> 94.6 us
    pallas_call x1, Pallas kernels: 101 us -> 94.6 us  [body(): pl.pallas_call(kernel, out_shape=jax.ShapeDtypeStruct((MB * ROWS, NC), f3...]
where the time goes in v3:
time: 97.8 us; the launch traced here: 97.7 us
  Pallas kernels  94.6 us (97%)
  local copies, waits for them, and re-layouts  3.05 us (3%)
    pallas_call x1, Pallas kernels, body(): pl.pallas_call(kernel, out_shape=jax.ShapeDtypeStruct((MB * ROWS, NC), f3...  94.6 us
    unnamed x1, local copies, waits for them, and re-layouts  3.05 us

profile of v3, /device:TPU:0, one launch (start us, length us, event | category | flops | bytes accessed | tf_op | source)
XLA Modules:
  0.0 97.7 jit_solution(2142804714112384114)
XLA Ops:
  0.0 94.6 %shard_map.55 = f32[4096,128]{1,0:T(8,128)} custom-call(f32[4096,128]{1,0:T(8,128)} %bitcast.4, f32[2,512]{1,0:T(2,128)} %courant.1, f32[1,512]{1,0:T(1,128)} %bitcast.5, s32[8,128]{1,0:T(8,128)} %flags.1, f32[512,4096]{1,0:T(8,128)} %weight.1), custom_call_target="tpu_custom_call" | custom-call | tf_op jit(solution)/shard_map/pallas_call | solution.py:450
  94.6 3.0 %copy.7 = f32[512,8,128]{2,1,0:T(8,128)} copy(f32[512,8,128]{2,1,0:T(8,128)} %bitcast.3) | data formatting | bytes 4194304
